TPU v7x, 32 devices: a whole 2x2x4 slice. The times are simulated.
32 devices in a mesh: refl: 4 (over y, x), grid: 8 (over z, core).
Axes of the slice: x: 2, y: 2, z: 4, core: 2. Of those that a mesh axis runs over, the one named last changes fastest.
Arguments:
- density: bfloat16 [2, 256, 256, 256], P(None, 'grid'), may hold values from -6 to 6
- displacement: bfloat16 [3, 256, 256, 256], P(None, 'grid'), may hold values from -0.8984375 to 0.8984375
- support: int32 [256, 256, 256], P('grid'), may hold values 0 or 1
- millers: int32 [4, 3], replicated, may hold values from -3 to 3
- amplitude: float32 [4, 256, 256, 256], P('refl', None, 'grid'), may hold values from 0.1 to 3
Outputs:
- grad_density: float32 [2, 256, 256, 256], P(None, 'grid', 'refl')
- grad_displacement: float32 [3, 256, 256, 256], P(None, 'grid', 'refl')
All inputs are finite; a program needn't handle non-finite values. No bound on the sum of `support` on one device may be relied on, other than what follows from the above.
Results may differ from a plain program's by a relative error of at most 0.00065.
Values sent between devices are 32-bit elements; how exact they have to be, the bound alone decides.
A program may use at most 192 MiB of HBM per device.

v0:
```python
import math
import jax
import jax.numpy as jnp
from jax import lax
from jax.sharding import PartitionSpec as P


def dft_tables(length):
    counter = jnp.arange(length, dtype=jnp.int32)
    product = counter[:, None] * counter[None, :] % length
    angles = product.astype(jnp.float32) * (2.0 * math.pi / length)
    factor = 1.0 / math.sqrt(length)
    return (jnp.cos(angles) * factor, jnp.sin(angles) * factor)


def transform_axis(real_part, imag_part, pattern, tables, inverse):
    cosine, sine = tables
    real_cos = jnp.einsum(pattern, real_part, cosine, precision=lax.Precision.HIGHEST)
    real_sin = jnp.einsum(pattern, real_part, sine, precision=lax.Precision.HIGHEST)
    imag_cos = jnp.einsum(pattern, imag_part, cosine, precision=lax.Precision.HIGHEST)
    imag_sin = jnp.einsum(pattern, imag_part, sine, precision=lax.Precision.HIGHEST)
    if inverse:
        return (real_cos - imag_sin, imag_cos + real_sin)
    return (real_cos + imag_sin, imag_cos - real_sin)


def phase_terms(hkl_rows, shift):
    angle = (
        2.0
        * math.pi
        * jnp.einsum("gc,cxyz->gxyz", hkl_rows, shift, precision=lax.Precision.HIGHEST)
    )
    return (jnp.cos(angle), jnp.sin(angle))


def gradient_terms(hkl_rows, mask, rho_real, rho_imag, cosine, sine, back_real, back_imag):
    obj_real = mask * (rho_real * cosine - rho_imag * sine)
    obj_imag = mask * (rho_real * sine + rho_imag * cosine)
    grad_real = jnp.sum(mask * (cosine * back_real + sine * back_imag), axis=0)
    grad_imag = jnp.sum(mask * (cosine * back_imag - sine * back_real), axis=0)
    twist = obj_real * back_imag - obj_imag * back_real
    grad_shift = jnp.einsum("gc,gxyz->cxyz", hkl_rows, twist, precision=lax.Precision.HIGHEST)
    return (jnp.stack([grad_real, grad_imag]), grad_shift)


def body(density, displacement, support, millers, amplitude):
    local_refl = amplitude.shape[0]
    total_refl = millers.shape[0]
    full_x = amplitude.shape[1]
    full_y = support.shape[1]
    full_z = support.shape[2]
    rho_real = density[0].astype(jnp.float32)
    rho_imag = density[1].astype(jnp.float32)
    shift = displacement.astype(jnp.float32)
    mask = support.astype(jnp.float32)
    indices = millers.astype(jnp.float32)
    table_x = dft_tables(full_x)
    table_y = dft_tables(full_y)
    table_z = dft_tables(full_z)
    first_refl = lax.axis_index("refl") * local_refl
    own_hkl = lax.dynamic_slice_in_dim(indices, first_refl, local_refl, 0)
    cosine, sine = phase_terms(own_hkl, shift)
    obj_real = mask * (rho_real * cosine - rho_imag * sine)
    obj_imag = mask * (rho_real * sine + rho_imag * cosine)
    real_part, imag_part = transform_axis(obj_real[0], obj_imag[0], "xyz,zk->xyk", table_z, False)
    real_part, imag_part = transform_axis(real_part, imag_part, "xyz,yk->xkz", table_y, False)
    columns = lax.all_to_all(
        jnp.stack([real_part, imag_part]), "grid", split_axis=2, concat_axis=1, tiled=True
    )
    spec_real, spec_imag = transform_axis(columns[0], columns[1], "xyz,xk->kyz", table_x, False)
    magnitude = jnp.sqrt(spec_real * spec_real + spec_imag * spec_imag)
    ratio = amplitude[0] / jnp.maximum(magnitude, 0.5)
    resid_real = spec_real - ratio * spec_real
    resid_imag = spec_imag - ratio * spec_imag
    real_part, imag_part = transform_axis(resid_real, resid_imag, "xyz,xk->kyz", table_x, True)
    slabs = lax.all_to_all(
        jnp.stack([real_part, imag_part]), "grid", split_axis=1, concat_axis=2, tiled=True
    )
    real_part, imag_part = transform_axis(slabs[0], slabs[1], "xyz,yk->xkz", table_y, True)
    real_part, imag_part = transform_axis(real_part, imag_part, "xyz,zk->xyk", table_z, True)
    back_reals = [real_part]
    back_imags = [imag_part]
    back_real = jnp.stack(back_reals)
    back_imag = jnp.stack(back_imags)
    scale = 1.0 / total_refl
    grad_rho, grad_shift = gradient_terms(
        own_hkl, mask, rho_real, rho_imag, cosine, sine, back_real, back_imag
    )
    grad_rho, grad_shift = (
        lax.psum_scatter(grad_rho, "refl", scatter_dimension=2, tiled=True),
        lax.psum_scatter(grad_shift, "refl", scatter_dimension=2, tiled=True),
    )
    return (grad_rho * scale, grad_shift * scale)


def solution(mesh):
    in_specs = (
        P(None, "grid", None, None),
        P(None, "grid", None, None),
        P("grid", None, None),
        P(),
        P("refl", None, "grid", None),
    )
    out_specs = (P(None, "grid", "refl", None), P(None, "grid", "refl", None))
    return jax.shard_map(body, mesh=mesh, in_specs=in_specs, out_specs=out_specs, check_vma=False)
```

profile of v0, /device:TPU:0, one launch (start us, length us, event | category | flops | bytes accessed | tf_op | source)
XLA Modules:
  0.0 1654.8 jit_solution(4140846365251873728)
XLA Ops:
  7.2 0.7 convert_element_type.71
  7.9 62.4 %fusion = f32[1,32,256,256]{3,0,2,1:T(1,128)} fusion(bf16[3,32,256,256]{3,2,1,0:T(8,128)(2,1)} %param.6, f32[4,3]{1,0:T(4,128)S(1)} %convert_element_type.71, s32[]{:T(128)S(6)} %select_n.60), kind=kOutput, calls=%fused_computation.5 | convolution fusion | flops 75497472 | bytes 20972036 | tf_op jit(solution)/shard_map/gc,cxyz->gxyz/dot_general | solution.py:31
  70.2 0.0 copy-done.6
  70.2 0.0 copy-done.4
  70.2 34.3 %fusion.3 = (f32[32,256,256]{2,1,0:T(8,128)S(1)}, f32[32,256,256]{2,1,0:T(8,128)S(1)}) fusion(s32[32,256,256]{2,1,0:T(8,128)S(1)} %copy-done.4, f32[1,32,256,256]{3,0,2,1:T(1,128)} %fusion, bf16[2,32,256,256]{3,2,1,0:T(8,128)(2,1)} %param.5), kind=kLoop, calls=%fused_computation.15 | loop fusion | flops 25165824 | bytes 41943040 | tf_op jit(solution)/shard_map/mul | solution.py:63
  104.5 0.0 copy-start.1
  104.5 0.0 copy-start
  104.6 7.9 fusion.68
  112.4 0.0 copy-done.1
  112.5 8.6 fusion.57
  121.0 8.3 fusion.55
  129.3 0.0 copy-done
  129.3 10.8 fusion.70
  140.2 11.6 fusion.22
  151.7 11.7 fusion.20
  163.5 17.8 %add_bitcast_fusion.1 = f32[1,32,256,256]{3,2,1,0:T(8,128)} fusion(f32[256,32,256]{2,0,1:T(8,128)} %fusion.22, f32[32,256,256]{2,1,0:T(8,128)} %fusion.70, f32[32,256,256]{2,1,0:T(8,128)S(1)} %fusion.57), kind=kOutput, calls=%fused_computation.34 | convolution fusion | flops 6447628288 | bytes 33554432 | tf_op jit(solution)/shard_map/xyz,yk->xkz/dot_general | solution.py:18
  181.3 18.4 %subtract_bitcast_fusion.1 = f32[1,32,256,256]{3,2,1,0:T(8,128)} fusion(f32[256,32,256]{2,0,1:T(8,128)} %fusion.20, f32[32,256,256]{2,1,0:T(8,128)} %fusion.70, f32[32,256,256]{2,1,0:T(8,128)S(1)} %fusion.57), kind=kOutput, calls=%fused_computation.33 | convolution fusion | flops 6447628288 | bytes 33554432 | tf_op jit(solution)/shard_map/xyz,yk->xkz/dot_general | solution.py:19
  199.7 6.9 pad_maximum_fusion
  206.6 17.6 %copy.32 = f32[2,32,256,256]{3,1,0,2:T(8,128)S(1)} copy(f32[2,32,256,256]{3,2,1,0:T(8,128)S(1)} %pad_maximum_fusion) | data formatting | bytes 33554432 | tf_op jit(solution)/shard_map/stack | solution.py:68
  224.2 370.7 %all_to_all.30 = f32[2,32,256,256]{3,1,0,2:T(8,128)S(1)} all-to-all(f32[2,32,256,256]{3,1,0,2:T(8,128)S(1)} %copy.32), channel_id=1, replica_groups=mesh['refl'=4,'grid'=8] {'grid'}, dimensions={2} | all-to-all | bytes 33554432 | tf_op jit(solution)/shard_map/all_to_all | solution.py:67
  594.9 6.0 copy.117
  601.0 6.8 fusion.205
  607.7 0.0 copy-start.2
  607.7 11.7 fusion.47
  619.4 11.6 fusion.73
  631.0 0.0 copy-done.2
  631.0 11.9 fusion.49
  642.9 23.2 %multiply_subtract_fusion.1 = (f32[256,32,256]{2,0,1:T(8,128)S(1)}, f32[256,32,256]{2,0,1:T(8,128)S(1)}) fusion(f32[1,256,32,256]{3,2,1,0:T(8,128)} %param.9, f32[256,32,256]{2,0,1:T(8,128)} %fusion.47, f32[256,32,256]{2,0,1:T(8,128)} %fusion.73, f32[256,32,256]{2,0,1:T(8,128)} %fusion.49, f32[256,32,256]{2,0,1:T(8,128)} %bitcast.191), kind=kOutput, calls=%fused_computation.9 | convolution fusion | flops 6466502656 | bytes 58720256 | tf_op jit(solution)/shard_map/xyz,xk->kyz/dot_general | solution.py:20
  666.1 12.1 fusion.75
  678.2 11.7 fusion.61
  689.9 14.1 subtract_bitcast_fusion
  703.9 14.1 add_bitcast_fusion
  718.0 0.0 copy-done.5
  718.0 4.9 pad_maximum_fusion.1
  722.9 20.2 %copy.43 = f32[2,256,32,256]{3,2,0,1:T(8,128)} copy(f32[2,256,32,256]{3,1,2,0:T(8,128)S(1)} %pad_maximum_fusion.1) | data formatting | bytes 33554432 | tf_op jit(solution)/shard_map/stack | solution.py:77
  743.2 5.7 all-to-all-start.1
  748.9 0.0 reduce-scatter.3.cloned.1.call-start
  749.0 1.0 fusion.232
  749.9 362.6 %all-to-all-done.1 = f32[2,256,32,256]{3,2,0,1:T(8,128)} async-done(((f32[2,256,32,256]{3,2,0,1:T(8,128)}), f32[2,256,32,256]{3,2,0,1:T(8,128)}, u32[]{:S(2)}, u32[]{:S(2)}) %all-to-all-start.1) | async-done | bytes 16777248 | tf_op jit(solution)/shard_map/all_to_all | solution.py:76
  1112.5 11.9 copy.116
  1124.4 7.9 fusion.204
  1132.4 0.0 copy-start.3
  1132.4 8.6 fusion.41
  1141.0 0.0 copy-done.3
  1141.0 8.8 fusion.59
  1149.9 10.8 fusion.6
  1160.7 11.0 fusion.8
  1171.8 11.7 fusion.43
  1183.4 14.2 fusion.77
  1197.6 15.6 fusion.32
  1213.2 0.0 slice-done
  1213.2 0.0 slice-done.2
  1213.2 0.0 slice-done.1
  1213.3 43.5 %multiply_bitcast_fusion.1 = (f32[1,32,256,256]{3,2,1,0:T(8,128)S(1)}, f32[1,32,256,256]{3,2,1,0:T(8,128)S(1)}, f32[32,256,256]{2,1,0:T(8,128)}) fusion(f32[32,256,256]{2,1,0:T(8,128)} %fusion.32, s32[32,256,256]{2,1,0:T(8,128)} %param.7, f32[1,32,256,256]{3,0,2,1:T(1,128)} %fusion, f32[32,256,256]{2,1,0:T(8,128)S(1)} %bitcast.189, ...), kind=kOutput, calls=%fused_computation.30 | convolution fusion | flops 6473908224 | bytes 92536832 | tf_op jit(solution)/shard_map/xyz,zk->xyk/dot_general | solution.py:19
  1256.7 6.4 pad_maximum_fusion.2
  1263.1 0.0 reduce-scatter.3.cloned.1.call-update
  1263.1 0.0 reduce-scatter.5.cloned.1.call-start
  1263.2 0.7 fusion.107
  1263.9 12.6 broadcast_multiply_fusion
  1276.4 0.0 reduce-scatter.5.cloned.1.call-update
  1276.5 139.5 %reduce-scatter.3.cloned.1.call-done = f32[2,32,64,256]{3,2,1,0:T(8,128)} async-done(((f32[2,32,256,256]{3,2,1,0:T(8,128)}), f32[2,32,64,256]{3,2,1,0:T(8,128)}) %reduce-scatter.3.cloned.1.call-update) | async-done | bytes 4194320 | tf_op jit(solution)/shard_map/reduce_scatter | solution.py:90
  1416.0 4.8 broadcast_multiply_fusion.2
  1420.8 220.1 %reduce-scatter.5.cloned.1.call-done = f32[3,32,64,256]{3,2,1,0:T(8,128)} async-done(((f32[3,32,256,256]{3,2,1,0:T(8,128)}), f32[3,32,64,256]{3,2,1,0:T(8,128)}) %reduce-scatter.5.cloned.1.call-update) | async-done | bytes 6291472 | tf_op jit(solution)/shard_map/reduce_scatter | solution.py:91
  1640.8 6.6 broadcast_multiply_fusion.1
  (10 shorter events, 0.0 us)
Async XLA Ops:
  7.9 62.4 %copy-start.6 = (f32[4,3]{1,0:T(4,128)}, f32[4,3]{1,0:T(4,128)S(1)}, u32[]{:S(2)}) copy-start(f32[4,3]{1,0:T(4,128)S(1)} %convert_element_type.71) | copy-start | bytes 148
  7.9 62.4 %copy-start.4 = (s32[32,256,256]{2,1,0:T(8,128)S(1)}, s32[32,256,256]{2,1,0:T(8,128)}, u32[]{:S(2)}) copy-start(s32[32,256,256]{2,1,0:T(8,128)} %param.7) | copy-start | bytes 25165828
  104.5 7.9 copy-start.1
  104.5 24.8 %copy-start = (f32[32,256,256]{2,1,0:T(8,128)}, f32[32,256,256]{2,1,0:T(8,128)S(1)}, u32[]{:S(2)}) copy-start(f32[32,256,256]{2,1,0:T(8,128)S(1)} %get-tuple-element.6) | copy-start | bytes 25165828
  607.7 23.3 %copy-start.2 = (f32[1,8,32,32,256]{4,2,1,3,0:T(8,128)}, f32[1,8,32,32,256]{4,2,1,3,0:T(8,128)S(1)}, u32[]{:S(2)}) copy-start(f32[1,8,32,32,256]{4,2,1,3,0:T(8,128)S(1)} %get-tuple-element.12) | copy-start | bytes 25165828
  703.9 14.1 copy-start.5
  743.2 369.4 %all-to-all-start.1 = ((f32[2,256,32,256]{3,2,0,1:T(8,128)}), f32[2,256,32,256]{3,2,0,1:T(8,128)}, u32[]{:S(2)}, u32[]{:S(2)}) async-start(f32[2,256,32,256]{3,2,0,1:T(8,128)} %copy.43), calls=%async_computation.1 | async-start | bytes 33554432 | tf_op jit(solution)/shard_map/all_to_all | solution.py:76
  748.9 667.0 %reduce-scatter.3.cloned.1.call-start = ((), (), s32[]{:S(2)}) async-start(), calls=%async_computation.4 | async-start | bytes 20971520 | tf_op jit(solution)/shard_map/reduce_scatter | solution.py:90
  1132.4 8.7 copy-start.3
  1183.4 29.8 %slice-start = ((s8[8388608]{0:T(1024)(128)(4,1)}), s8[4194304]{0:T(1024)(128)(4,1)S(1)}, s32[]{:S(2)}) async-start(s8[8388608]{0:T(1024)(128)(4,1)} %bitcast.186), calls=%async_computation.6 | async-start | bytes 8388608
  1183.4 29.8 %slice-start.2 = ((s8[8388608]{0:T(1024)(128)(4,1)}), s8[4194304]{0:T(1024)(128)(4,1)S(1)}, s32[]{:S(2)}) async-start(s8[8388608]{0:T(1024)(128)(4,1)} %bitcast.188), calls=%async_computation.8 | async-start | bytes 8388608
  1197.6 15.6 slice-start.1
  1197.6 15.6 slice-start.3
  1263.1 377.7 %reduce-scatter.5.cloned.1.call-start = ((), (), s32[]{:S(2)}) async-start(), calls=%async_computation.5 | async-start | bytes 31457280 | tf_op jit(solution)/shard_map/reduce_scatter | solution.py:91
Sparse Core Ops, SparseCore 0:
  1263.3 152.6 reduce-scatter.2
  1419.1 221.7 reduce-scatter.4
where the time goes:
time: 1660 us; the launch traced here: 1650 us
  waiting for transfers between devices  722 us (43%)
  matrix products  392 us (24%)
  blocking collectives  371 us (22%)
  other arithmetic  78.1 us (5%)
  local copies, waits for them, and re-layouts  71.2 us (4%)
    all_to_all x1, blocking collectives, body(): lax.all_to_all(jnp.stack([real_part, imag_part]), 'grid', split_axis=2, c...  371 us
    all_to_all x1, waiting for transfers between devices, body(): lax.all_to_all(jnp.stack([real_part, imag_part]), 'grid', split_axis=1, c...  363 us
    reduce_scatter x1, waiting for transfers between devices, body(): lax.psum_scatter(grad_shift, 'refl', scatter_dimension=2, tiled=True)  220 us
    reduce_scatter x1, waiting for transfers between devices, body(): lax.psum_scatter(grad_rho, 'refl', scatter_dimension=2, tiled=True)  139 us
    dot_general x6, matrix products, transform_axis(): jnp.einsum(pattern, real_part, sine, precision=lax.Precision.HIGHEST)  105 us
    dot_general x6, matrix products, transform_axis(): jnp.einsum(pattern, real_part, cosine, precision=lax.Precision.HIGHEST)  82.2 us
    dot_general x6, matrix products, transform_axis(): jnp.einsum(pattern, imag_part, cosine, precision=lax.Precision.HIGHEST)  74.2 us
    dot_general x6, matrix products, transform_axis(): jnp.einsum(pattern, imag_part, sine, precision=lax.Precision.HIGHEST)  68.7 us
  transfers between devices with their start and end apart: 3, of which 3 were waited for; matrix products, arithmetic and copies ran while one was open for 1% of the time, Pallas kernels for 0%

commit v1 on v0

--- a/solution.py
+++ b/solution.py
@@ -73,9 +73,16 @@
     resid_real = spec_real - ratio * spec_real
     resid_imag = spec_imag - ratio * spec_imag
     real_part, imag_part = transform_axis(resid_real, resid_imag, "xyz,xk->kyz", table_x, True)
-    slabs = lax.all_to_all(
-        jnp.stack([real_part, imag_part]), "grid", split_axis=1, concat_axis=2, tiled=True
+    pack_patch = lambda incoming_x: jnp.concatenate(
+        lax.all_to_all(
+            jnp.stack(jnp.split(incoming_x, lax.axis_size("grid"), 1), axis=0),
+            axis_name="grid",
+            split_axis=0,
+            concat_axis=0,
+        ),
+        2,
     )
+    slabs = pack_patch(jnp.stack([real_part, imag_part]))
     real_part, imag_part = transform_axis(slabs[0], slabs[1], "xyz,yk->xkz", table_y, True)
     real_part, imag_part = transform_axis(real_part, imag_part, "xyz,zk->xyk", table_z, True)
     back_reals = [real_part]

time: 1660 us -> 1620 us (0.976)
  local copies, waits for them, and re-layouts: 71.2 us -> 38.9 us
    dot_general x1, matrix products: 62.4 us -> 37 us  [phase_terms(): jnp.einsum('gc,cxyz->gxyz', hkl_rows, shift, precision=lax.Precision.HIGH...]
    another operation x2 -> x1, local copies, waits for them, and re-layouts: 37.9 us -> 17.6 us  [body(): jnp.stack([real_part, imag_part])]
where the time goes in v1:
time: 1620 us; the launch traced here: 1610 us
  waiting for transfers between devices  722 us (45%)
  matrix products  376 us (23%)
  blocking collectives  371 us (23%)
  other arithmetic  84.6 us (5%)
  local copies, waits for them, and re-layouts  38.9 us (2%)
    all_to_all x1, blocking collectives, body(): lax.all_to_all(jnp.stack([real_part, imag_part]), 'grid', split_axis=2, c...  371 us
    all_to_all x1, waiting for transfers between devices, body(): lax.all_to_all(jnp.stack(jnp.split(incoming_x, lax.axis_size('grid'), 1),...  363 us
    reduce_scatter x1, waiting for transfers between devices, body(): lax.psum_scatter(grad_shift, 'refl', scatter_dimension=2, tiled=True)  220 us
    reduce_scatter x1, waiting for transfers between devices, body(): lax.psum_scatter(grad_rho, 'refl', scatter_dimension=2, tiled=True)  139 us
    dot_general x6, matrix products, transform_axis(): jnp.einsum(pattern, real_part, sine, precision=lax.Precision.HIGHEST)  107 us
    dot_general x6, matrix products, transform_axis(): jnp.einsum(pattern, real_part, cosine, precision=lax.Precision.HIGHEST)  82.5 us
    dot_general x6, matrix products, transform_axis(): jnp.einsum(pattern, imag_part, cosine, precision=lax.Precision.HIGHEST)  78.4 us
    dot_general x6, matrix products, transform_axis(): jnp.einsum(pattern, imag_part, sine, precision=lax.Precision.HIGHEST)  71 us
  transfers between devices with their start and end apart: 3, of which 3 were waited for; matrix products, arithmetic and copies ran while one was open for 1% of the time, Pallas kernels for 0%

profile of v1, /device:TPU:0, one launch (start us, length us, event | category | flops | bytes accessed | tf_op | source)
XLA Modules:
  0.0 1613.6 jit_solution(15317771073000106770)
XLA Ops:
  7.2 0.7 convert_element_type.71
  7.9 37.0 %fusion = f32[1,32,256,256]{3,0,2,1:T(1,128)S(1)} fusion(bf16[3,32,256,256]{3,2,1,0:T(8,128)(2,1)} %param.6, f32[4,3]{1,0:T(4,128)S(1)} %convert_element_type.71, s32[]{:T(128)S(6)} %select_n.60), kind=kOutput, calls=%fused_computation.17 | convolution fusion | flops 75497472 | bytes 20972036 | tf_op jit(solution)/shard_map/gc,cxyz->gxyz/dot_general | solution.py:31
  44.9 0.0 copy-done.9
  44.9 0.0 copy-done.7
  44.9 0.0 copy-start.8
  44.9 34.0 %fusion.3 = (f32[32,256,256]{2,1,0:T(8,128)S(1)}, f32[32,256,256]{2,1,0:T(8,128)S(1)}) fusion(s32[32,256,256]{2,1,0:T(8,128)S(1)} %copy-done.7, f32[1,32,256,256]{3,0,2,1:T(1,128)S(1)} %fusion, bf16[2,32,256,256]{3,2,1,0:T(8,128)(2,1)} %param.5), kind=kLoop, calls=%fused_computation.27 | loop fusion | flops 25165824 | bytes 41943040 | tf_op jit(solution)/shard_map/mul | solution.py:63
  78.9 0.0 copy-done.8
  78.9 0.0 copy-start.1
  78.9 0.0 copy-start
  79.0 7.9 fusion.96
  86.8 0.0 copy-done.1
  86.9 8.3 fusion.86
  95.2 8.5 fusion.84
  103.8 10.8 fusion.98
  114.6 11.6 fusion.30
  126.2 11.7 fusion.28
  137.9 17.8 %add_bitcast_fusion.1 = f32[1,32,256,256]{3,2,1,0:T(8,128)} fusion(f32[256,32,256]{2,0,1:T(8,128)} %fusion.30, f32[32,256,256]{2,1,0:T(8,128)} %fusion.98, f32[32,256,256]{2,1,0:T(8,128)S(1)} %fusion.86), kind=kOutput, calls=%fused_computation.46 | convolution fusion | flops 6447628288 | bytes 33554432 | tf_op jit(solution)/shard_map/xyz,yk->xkz/dot_general | solution.py:18
  155.6 18.1 %subtract_bitcast_fusion.1 = f32[1,32,256,256]{3,2,1,0:T(8,128)} fusion(f32[256,32,256]{2,0,1:T(8,128)} %fusion.28, f32[32,256,256]{2,1,0:T(8,128)} %fusion.98, f32[32,256,256]{2,1,0:T(8,128)S(1)} %fusion.86), kind=kOutput, calls=%fused_computation.45 | convolution fusion | flops 6447628288 | bytes 33554432 | tf_op jit(solution)/shard_map/xyz,yk->xkz/dot_general | solution.py:19
  173.8 6.9 pad_maximum_fusion
  180.6 17.6 %copy.34 = f32[2,32,256,256]{3,1,0,2:T(8,128)S(1)} copy(f32[2,32,256,256]{3,2,1,0:T(8,128)S(1)} %pad_maximum_fusion) | data formatting | bytes 33554432 | tf_op jit(solution)/shard_map/stack | solution.py:68
  198.3 371.0 %all_to_all.20 = f32[2,32,256,256]{3,1,0,2:T(8,128)S(1)} all-to-all(f32[2,32,256,256]{3,1,0,2:T(8,128)S(1)} %copy.34), channel_id=1, replica_groups=mesh['refl'=4,'grid'=8] {'grid'}, dimensions={2} | all-to-all | bytes 33554432 | tf_op jit(solution)/shard_map/all_to_all | solution.py:67
  569.3 6.1 copy.127
  575.3 6.8 fusion.232
  582.1 11.7 fusion.101
  593.8 11.6 fusion.76
  605.5 11.9 fusion.78
  617.4 23.2 %multiply_subtract_fusion = (f32[256,32,256]{2,0,1:T(8,128)S(1)}, f32[256,32,256]{2,0,1:T(8,128)S(1)}) fusion(f32[1,256,32,256]{3,2,1,0:T(8,128)} %param.9, f32[256,32,256]{2,0,1:T(8,128)} %fusion.76, f32[256,32,256]{2,0,1:T(8,128)} %fusion.101, f32[256,32,256]{2,0,1:T(8,128)} %fusion.78, f32[256,32,256]{2,0,1:T(8,128)} %bitcast.216), kind=kOutput, calls=%fused_computation.20 | convolution fusion | flops 6466502656 | bytes 58720256 | tf_op jit(solution)/shard_map/xyz,xk->kyz/dot_general | solution.py:20
  640.5 12.0 fusion.89
  652.5 0.0 copy-done.2
  652.5 11.8 fusion.103
  664.2 12.8 add_bitcast_fusion
  677.1 13.7 subtract_bitcast_fusion
  690.8 1.5 fusion.51
  692.3 1.5 fusion.54
  693.8 1.4 fusion.57
  695.2 1.5 fusion.60
  696.7 1.4 fusion.63
  698.1 1.5 fusion.66
  699.6 1.4 fusion.48
  701.0 1.5 fusion.68
  702.5 5.8 all-to-all-start.1
  708.3 0.0 reduce-scatter.3.cloned.1.call-start
  708.4 1.0 fusion.255
  709.4 362.6 %all-to-all-done.1 = f32[8,2,32,32,256]{4,2,3,1,0:T(8,128)} async-done(((f32[8,2,32,32,256]{4,2,3,1,0:T(8,128)}), f32[8,2,32,32,256]{4,2,3,1,0:T(8,128)}, u32[]{:S(2)}, u32[]{:S(2)}) %all-to-all-start.1) | async-done | bytes 16777248 | tf_op jit(solution)/shard_map/all_to_all | solution.py:77
  1072.0 7.7 fusion.231
  1079.7 12.9 fusion.14
  1092.6 12.8 fusion.18
  1105.4 0.0 slice-start.4
  1105.4 10.8 fusion.6
  1116.2 10.8 fusion.8
  1127.1 14.7 fusion.16
  1141.8 14.8 fusion.20
  1156.6 15.6 fusion.40
  1172.3 43.4 %multiply_bitcast_fusion.1 = (f32[1,32,256,256]{3,2,1,0:T(8,128)S(1)}, f32[1,32,256,256]{3,2,1,0:T(8,128)S(1)}, f32[32,256,256]{2,1,0:T(8,128)}) fusion(f32[32,256,256]{2,1,0:T(8,128)} %fusion.40, s32[32,256,256]{2,1,0:T(8,128)} %param.7, f32[1,32,256,256]{3,0,2,1:T(1,128)} %copy-done.8, f32[32,256,256]{2,1,0:T(8,128)S(1)} %bitcast.214, ...), kind=kOutput, calls=%fused_computation.42 | convolution fusion | flops 6473908224 | bytes 92536832 | tf_op jit(solution)/shard_map/xyz,zk->xyk/dot_general | solution.py:19
  1215.7 6.4 pad_maximum_fusion.1
  1222.0 0.0 reduce-scatter.3.cloned.1.call-update
  1222.1 0.0 reduce-scatter.5.cloned.1.call-start
  1222.1 0.7 fusion.134
  1222.8 12.6 broadcast_multiply_fusion
  1235.4 0.0 reduce-scatter.5.cloned.1.call-update
  1235.4 139.5 %reduce-scatter.3.cloned.1.call-done = f32[2,32,64,256]{3,2,1,0:T(8,128)} async-done(((f32[2,32,256,256]{3,2,1,0:T(8,128)}), f32[2,32,64,256]{3,2,1,0:T(8,128)}) %reduce-scatter.3.cloned.1.call-update) | async-done | bytes 4194320 | tf_op jit(solution)/shard_map/reduce_scatter | solution.py:97
  1374.9 4.8 broadcast_multiply_fusion.2
  1379.7 220.1 %reduce-scatter.5.cloned.1.call-done = f32[3,32,64,256]{3,2,1,0:T(8,128)} async-done(((f32[3,32,256,256]{3,2,1,0:T(8,128)}), f32[3,32,64,256]{3,2,1,0:T(8,128)}) %reduce-scatter.5.cloned.1.call-update) | async-done | bytes 6291472 | tf_op jit(solution)/shard_map/reduce_scatter | solution.py:98
  1599.7 6.6 broadcast_multiply_fusion.1
  (26 shorter events, 0.0 us)
Async XLA Ops:
  7.9 37.0 %copy-start.9 = (f32[4,3]{1,0:T(4,128)}, f32[4,3]{1,0:T(4,128)S(1)}, u32[]{:S(2)}) copy-start(f32[4,3]{1,0:T(4,128)S(1)} %convert_element_type.71) | copy-start | bytes 148
  7.9 37.0 %copy-start.7 = (s32[32,256,256]{2,1,0:T(8,128)S(1)}, s32[32,256,256]{2,1,0:T(8,128)}, u32[]{:S(2)}) copy-start(s32[32,256,256]{2,1,0:T(8,128)} %param.7) | copy-start | bytes 25165828
  44.9 34.0 %copy-start.8 = (f32[1,32,256,256]{3,0,2,1:T(1,128)}, f32[1,32,256,256]{3,0,2,1:T(1,128)S(1)}, u32[]{:S(2)}) copy-start(f32[1,32,256,256]{3,0,2,1:T(1,128)S(1)} %fusion) | copy-start | bytes 25165828
  78.9 7.9 copy-start.1
  78.9 24.8 %copy-start = (f32[32,256,256]{2,1,0:T(8,128)}, f32[32,256,256]{2,1,0:T(8,128)S(1)}, u32[]{:S(2)}) copy-start(f32[32,256,256]{2,1,0:T(8,128)S(1)} %get-tuple-element.6) | copy-start | bytes 25165828
  582.1 23.4 %copy-start.3 = (f32[1,8,32,32,256]{4,2,1,3,0:T(8,128)}, f32[1,8,32,32,256]{4,2,1,3,0:T(8,128)S(1)}, u32[]{:S(2)}) copy-start(f32[1,8,32,32,256]{4,2,1,3,0:T(8,128)S(1)} %get-tuple-element.12) | copy-start | bytes 25165828
  640.5 12.0 copy-start.2
  702.5 369.4 %all-to-all-start.1 = ((f32[8,2,32,32,256]{4,2,3,1,0:T(8,128)}), f32[8,2,32,32,256]{4,2,3,1,0:T(8,128)}, u32[]{:S(2)}, u32[]{:S(2)}) async-start(f32[8,2,32,32,256]{4,2,3,1,0:T(8,128)} %fusion.68), calls=%async_computation.1 | async-start | bytes 33554432 | tf_op jit(solution)/shard_map/all_to_all | solution.py:77
  708.3 666.6 %reduce-scatter.3.cloned.1.call-start = ((), (), s32[]{:S(2)}) async-start(), calls=%async_computation.4 | async-start | bytes 20971520 | tf_op jit(solution)/shard_map/reduce_scatter | solution.py:97
  1079.7 12.9 copy-start.6
  1079.7 12.9 copy-start.4
  1105.4 21.7 %slice-start.4 = ((s8[8388608]{0:T(1024)(128)(4,1)}), s8[4194304]{0:T(1024)(128)(4,1)S(1)}, s32[]{:S(2)}) async-start(s8[8388608]{0:T(1024)(128)(4,1)} %bitcast.220), calls=%async_computation.10 | async-start | bytes 8388608
  1116.2 10.8 slice-start.5
  1127.1 14.7 copy-start.5
  1141.8 30.5 %slice-start = ((s8[8388608]{0:T(1024)(128)(4,1)}), s8[4194304]{0:T(1024)(128)(4,1)S(1)}, s32[]{:S(2)}) async-start(s8[8388608]{0:T(1024)(128)(4,1)} %bitcast.211), calls=%async_computation.6 | async-start | bytes 8388608
  1141.8 30.5 %slice-start.2 = ((s8[8388608]{0:T(1024)(128)(4,1)}), s8[4194304]{0:T(1024)(128)(4,1)S(1)}, s32[]{:S(2)}) async-start(s8[8388608]{0:T(1024)(128)(4,1)} %bitcast.213), calls=%async_computation.8 | async-start | bytes 8388608
  1156.6 15.6 slice-start.1
  1156.6 15.6 slice-start.3
  1222.1 377.7 %reduce-scatter.5.cloned.1.call-start = ((), (), s32[]{:S(2)}) async-start(), calls=%async_computation.5 | async-start | bytes 31457280 | tf_op jit(solution)/shard_map/reduce_scatter | solution.py:98
Sparse Core Ops, SparseCore 0:
  1222.2 152.6 reduce-scatter.2
  1378.0 221.7 reduce-scatter.4
